TPU v7x, 32 devices: a whole 2x2x4 slice. The times are simulated.
32 devices in a mesh: fsdp: 4 (over z), ctx: 2 (over x), tp: 4 (over y, core).
Axes of the slice: x: 2, y: 2, z: 4, core: 2. Of those that a mesh axis runs over, the one named last changes fastest.
Arguments:
- tokens: bfloat16 [4, 2048, 2048], P('fsdp', 'ctx'), may hold values from -6 to 6
- segments: int32 [4, 2048], P('fsdp'), may hold values from 0 to 7, never falling along the last dimension, each value on 1 to 1024 neighbouring positions
- cotangent: bfloat16 [4, 2048, 2048], P('fsdp', 'ctx'), may hold values from -6 to 6
- gain_mix: float32 [2048], replicated, may hold values from 0.5 to 1.5
- w_branch: bfloat16 [2048, 2560], P('fsdp', 'tp'), may hold values from -0.125 to 0.125
- w_input: bfloat16 [2048, 2560], P('fsdp', 'tp'), may hold values from -0.125 to 0.125
- conv_weight: float32 [4, 2560], P(None, 'tp'), may hold values from -3 to 3
- conv_bias: float32 [2560], P('tp'), may hold values from -1.75 to 1.75
- gate_a: bfloat16 [16, 160, 160], P('tp'), may hold values from -0.5 to 0.5
- bias_a: float32 [2560], P('tp'), may hold values from -3 to 3
- gate_x: bfloat16 [16, 160, 160], P('tp'), may hold values from -0.5 to 0.5
- bias_x: float32 [2560], P('tp'), may hold values from -3 to 3
- decay_param: float32 [2560], P('tp'), may hold values from 4 to 8
- w_out: bfloat16 [2560, 2048], P('tp', 'fsdp'), may hold values from -0.3125 to 0.3125
- gain_mlp: float32 [2048], replicated, may hold values from 0.5 to 1.5
- w_gate: bfloat16 [2048, 6144], P('fsdp', 'tp'), may hold values from -0.125 to 0.125
- w_up: bfloat16 [2048, 6144], P('fsdp', 'tp'), may hold values from -0.125 to 0.125
- w_down: bfloat16 [6144, 2048], P('tp', 'fsdp'), may hold values from -0.15625 to 0.15625
Outputs:
- output: bfloat16 [4, 2048, 2048], P('fsdp', 'ctx')
- grad_tokens: bfloat16 [4, 2048, 2048], P('fsdp', 'ctx')
- grad_gain_mix: float32 [2048], replicated
- grad_w_branch: float32 [2048, 2560], P('fsdp', 'tp')
- grad_w_input: float32 [2048, 2560], P('fsdp', 'tp')
- grad_conv_weight: float32 [4, 2560], P(None, 'tp')
- grad_conv_bias: float32 [2560], P('tp')
- grad_gate_a: float32 [16, 160, 160], P('tp')
- grad_bias_a: float32 [2560], P('tp')
- grad_gate_x: float32 [16, 160, 160], P('tp')
- grad_bias_x: float32 [2560], P('tp')
- grad_decay_param: float32 [2560], P('tp')
- grad_w_out: float32 [2560, 2048], P('tp', 'fsdp')
- grad_gain_mlp: float32 [2048], replicated
- grad_w_gate: float32 [2048, 6144], P('fsdp', 'tp')
- grad_w_up: float32 [2048, 6144], P('fsdp', 'tp')
- grad_w_down: float32 [6144, 2048], P('tp', 'fsdp')
Inputs may be any that keep to these rules, and one draw needn't show every extreme that they name: `segments`: within a sequence the document numbers never fall; every document has 1 to 1024 positions and one has exactly 1024.
All inputs are finite; a program needn't handle non-finite values.
Results may differ from a plain program's by a relative error of at most 0.012.
Values may be sent and summed in bfloat16 or wider, within the bound.
A program may use at most 256 MiB of HBM per device.

v0:
```python
import jax
import jax.numpy as jnp
from jax import lax
from jax.sharding import PartitionSpec as P

EPSILON = 1e-06
RATE_SCALE = 8.0


def passed_along(block, axis, distance):
    devices = range(lax.axis_size(axis))
    route = [(i - distance, i) for i in devices if i - distance in devices]
    return lax.ppermute(block, axis, route)


def entering_2(x, axis, combine, identity, reverse):
    length, place = (lax.axis_size(axis), lax.axis_index(axis))
    everything = jax.tree.map(lambda part: lax.all_gather(part, axis), x)
    start = jax.tree.map(
        lambda part, zero: jnp.broadcast_to(jnp.asarray(zero, part.dtype), part.shape), x, identity
    )

    def turn(k, before):
        at = length - 1 - k if reverse else k
        reached = at > place if reverse else at < place
        new = combine(before, jax.tree.map(lambda part: part[at], everything))
        return jax.tree.map(lambda a, b: jnp.where(reached, a, b), new, before)

    return lax.fori_loop(0, length, turn, start)


def linear_combine(earlier, later):
    return (earlier[0] * later[0], later[0] * earlier[1] + later[1])


def matmul(left, right):
    return jnp.dot(left, right, preferred_element_type=jnp.float32)


def left_inner(left, right):
    return lax.dot_general(
        left, right, (((0,), (0,)), ((), ())), preferred_element_type=jnp.float32
    )


def right_inner(left, right):
    return lax.dot_general(
        left, right, (((1,), (1,)), ((), ())), preferred_element_type=jnp.float32
    )


def gelu_slope(values):
    result, pull_back = jax.vjp(lambda inner_v: jax.nn.gelu(inner_v, approximate=True), values)
    return (result, pull_back(jnp.ones_like(values))[0])


def rms_rows(values):
    return lax.rsqrt(jnp.mean(values * values, axis=-1, keepdims=True) + EPSILON)


def norm_back(grad_norm, scaled, scale_row, gain):
    grad_scaled = grad_norm * gain
    return scale_row * (
        grad_scaled - scaled * jnp.mean(grad_scaled * scaled, axis=-1, keepdims=True)
    )


def shards(
    tokens,
    segments,
    cotangent,
    gain_mix,
    w_branch,
    w_input,
    conv_weight,
    conv_bias,
    gate_a,
    bias_a,
    gate_x,
    bias_x,
    decay_param,
    w_out,
    gain_mlp,
    w_gate,
    w_up,
    w_down,
):
    full_branch, full_input, full_gate, full_up, full_out, full_down = (
        lax.all_gather(w_branch, "fsdp", axis=0, tiled=True),
        lax.all_gather(w_input, "fsdp", axis=0, tiled=True),
        lax.all_gather(w_gate, "fsdp", axis=0, tiled=True),
        lax.all_gather(w_up, "fsdp", axis=0, tiled=True),
        lax.all_gather(w_out, "fsdp", axis=1, tiled=True),
        lax.all_gather(w_down, "fsdp", axis=1, tiled=True),
    )
    seq_count, tok_count, model_width = tokens.shape
    row_count = seq_count * tok_count
    kernel = conv_weight.shape[0]
    lag_rows = kernel - 1
    local_width = conv_bias.shape[0]
    head_count = gate_a.shape[0]
    block_width = gate_a.shape[1]
    inputs = tokens.reshape(row_count, model_width).astype(jnp.float32)
    scale_mix = rms_rows(inputs)
    scaled_mix = inputs * scale_mix
    normed = (scaled_mix * gain_mix).astype(jnp.bfloat16)
    branch_pre = matmul(normed, full_branch)
    branch, branch_slope = gelu_slope(branch_pre)
    conv_in = (
        matmul(normed, full_input).astype(jnp.bfloat16).reshape(seq_count, tok_count, local_width)
    )
    first_pos = lax.axis_index("ctx") * tok_count
    padded_seg = jnp.pad(segments, ((0, 0), (lag_rows, lag_rows)), constant_values=-1)
    near_seg = lax.dynamic_slice_in_dim(padded_seg, first_pos, tok_count + 2 * lag_rows, 1)
    own_seg = near_seg[:, lag_rows : lag_rows + tok_count]
    same_back = [
        near_seg[:, lag_rows - offset : lag_rows - offset + tok_count] == own_seg
        for offset in range(kernel)
    ]
    same_ahead = [
        near_seg[:, lag_rows + offset : lag_rows + offset + tok_count] == own_seg
        for offset in range(kernel)
    ]
    tail_rows = passed_along(conv_in[:, tok_count - lag_rows :], "ctx", 1)
    conv_ext = jnp.concatenate([tail_rows, conv_in], axis=1)
    conv_sum = jnp.zeros((seq_count, tok_count, local_width), jnp.float32) + conv_bias
    for offset in range(kernel):
        earlier_in = jnp.where(
            same_back[offset][..., None],
            conv_ext[:, lag_rows - offset : lag_rows - offset + tok_count],
            0.0,
        )
        conv_sum = conv_sum + conv_weight[offset] * earlier_in
    conv_out = conv_sum.astype(jnp.bfloat16)
    conv_heads = conv_out.reshape(seq_count, tok_count, head_count, block_width)
    pre_a = (
        jnp.einsum(
            "sthi,hij->sthj", conv_heads, gate_a, preferred_element_type=jnp.float32
        ).reshape(seq_count, tok_count, local_width)
        + bias_a
    )
    pre_x = (
        jnp.einsum(
            "sthi,hij->sthj", conv_heads, gate_x, preferred_element_type=jnp.float32
        ).reshape(seq_count, tok_count, local_width)
        + bias_x
    )
    recur_gate = jax.nn.sigmoid(pre_a)
    input_gate = jax.nn.sigmoid(pre_x)
    softened = jax.nn.softplus(-decay_param)
    log_decay = -RATE_SCALE * softened * recur_gate
    decay = jnp.exp(log_decay)
    root_term = jnp.sqrt(-jnp.expm1(2.0 * log_decay))
    starts = jnp.logical_not(same_back[1])[..., None]
    multiplier = jnp.where(starts, 1.0, root_term)
    carry_factor = jnp.where(starts, 0.0, decay)
    conv_float = conv_out.astype(jnp.float32)
    driven = input_gate * conv_float * multiplier
    decay_run, local_states = lax.associative_scan(linear_combine, (carry_factor, driven), axis=1)
    ones_state = jnp.ones((seq_count, local_width), jnp.float32)
    zero_state = jnp.zeros((seq_count, local_width), jnp.float32)
    entering = entering_2(
        (decay_run[:, -1], local_states[:, -1]),
        "ctx",
        linear_combine,
        (ones_state, zero_state),
        False,
    )[1]
    states = local_states + decay_run * entering[:, None]
    states_rows = states.reshape(row_count, local_width)
    mixed_out = (states_rows * branch).astype(jnp.bfloat16)
    mixer_term = matmul(mixed_out, full_out)
    resid_rows = inputs + lax.psum(mixer_term, "tp")
    scale_mlp = rms_rows(resid_rows)
    scaled_mlp = resid_rows * scale_mlp
    normed_mlp = (scaled_mlp * gain_mlp).astype(jnp.bfloat16)
    gate_pre = matmul(normed_mlp, full_gate)
    up_pre = matmul(normed_mlp, full_up)
    gate_act, gate_slope = gelu_slope(gate_pre)
    hidden = (gate_act * up_pre).astype(jnp.bfloat16)
    down_term = matmul(hidden, full_down)
    output = (resid_rows + lax.psum(down_term, "tp")).astype(jnp.bfloat16)
    grad_low = cotangent.reshape(row_count, model_width)
    grad_out = grad_low.astype(jnp.float32)
    grad_w_down = left_inner(hidden, grad_low)
    grad_hidden = right_inner(grad_low, full_down)
    grad_gate = (grad_hidden * up_pre * gate_slope).astype(jnp.bfloat16)
    grad_up = (grad_hidden * gate_act).astype(jnp.bfloat16)
    grad_w_gate = left_inner(normed_mlp, grad_gate)
    grad_w_up = left_inner(normed_mlp, grad_up)
    mlp_back_term = right_inner(grad_gate, full_gate) + right_inner(grad_up, full_up)
    grad_norm_mlp = lax.psum(mlp_back_term, "tp")
    grad_resid = grad_out + norm_back(grad_norm_mlp, scaled_mlp, scale_mlp, gain_mlp)
    grad_proj = grad_resid.astype(jnp.bfloat16)
    grad_gain_mlp = jnp.sum(grad_norm_mlp * scaled_mlp, axis=0)
    grad_w_out = left_inner(mixed_out, grad_proj)
    grad_mixed = right_inner(grad_proj, full_out)
    grad_branch = (grad_mixed * states_rows * branch_slope).astype(jnp.bfloat16)
    grad_states = (grad_mixed * branch).reshape(seq_count, tok_count, local_width)
    next_factor = jnp.concatenate(
        [carry_factor[:, 1:], jnp.ones((seq_count, 1, local_width), jnp.float32)], axis=1
    )
    run_back, local_back = lax.associative_scan(
        linear_combine, (jnp.flip(next_factor, 1), jnp.flip(grad_states, 1)), axis=1
    )
    run_back = jnp.flip(run_back, 1)
    local_back = jnp.flip(local_back, 1)
    leaving = (carry_factor[:, 0] * run_back[:, 0], carry_factor[:, 0] * local_back[:, 0])
    arriving = entering_2(leaving, "ctx", linear_combine, (ones_state, zero_state), True)[1]
    grad_total = local_back + run_back * arriving[:, None]
    prev_states = jnp.concatenate([entering[:, None], states[:, :-1]], axis=1)
    grad_mult = grad_total * input_gate * conv_float
    grad_log = jnp.where(
        starts, 0.0, grad_total * prev_states * decay - grad_mult * decay * decay / root_term
    )
    grad_decay_param = (
        RATE_SCALE * jax.nn.sigmoid(-decay_param) * jnp.sum(grad_log * recur_gate, axis=(0, 1))
    )
    grad_pre_a = (grad_log * (-RATE_SCALE * softened) * recur_gate * (1.0 - recur_gate)).astype(
        jnp.bfloat16
    )
    grad_pre_x = (grad_total * conv_float * multiplier * input_gate * (1.0 - input_gate)).astype(
        jnp.bfloat16
    )
    heads_a = grad_pre_a.reshape(seq_count, tok_count, head_count, block_width)
    heads_x = grad_pre_x.reshape(seq_count, tok_count, head_count, block_width)
    grad_gate_a = jnp.einsum(
        "sthi,sthj->hij", conv_heads, heads_a, preferred_element_type=jnp.float32
    )
    grad_gate_x = jnp.einsum(
        "sthi,sthj->hij", conv_heads, heads_x, preferred_element_type=jnp.float32
    )
    grad_bias_a = jnp.sum(grad_pre_a.astype(jnp.float32), axis=(0, 1))
    grad_bias_x = jnp.sum(grad_pre_x.astype(jnp.float32), axis=(0, 1))
    gate_back = jnp.einsum(
        "sthj,hij->sthi", heads_a, gate_a, preferred_element_type=jnp.float32
    ) + jnp.einsum("sthj,hij->sthi", heads_x, gate_x, preferred_element_type=jnp.float32)
    grad_conv = grad_total * input_gate * multiplier + gate_back.reshape(
        seq_count, tok_count, local_width
    )
    head_rows = passed_along(grad_conv[:, :lag_rows], "ctx", -1)
    grad_ext = jnp.concatenate([grad_conv, head_rows], axis=1)
    grad_conv_in = jnp.zeros((seq_count, tok_count, local_width), jnp.float32)
    weight_rows = []
    for offset in range(kernel):
        later_grad = jnp.where(
            same_ahead[offset][..., None], grad_ext[:, offset : offset + tok_count], 0.0
        )
        grad_conv_in = grad_conv_in + conv_weight[offset] * later_grad
        earlier_in = jnp.where(
            same_back[offset][..., None],
            conv_ext[:, lag_rows - offset : lag_rows - offset + tok_count],
            0.0,
        )
        weight_rows.append(jnp.sum(grad_conv * earlier_in, axis=(0, 1)))
    grad_conv_weight = jnp.stack(weight_rows)
    grad_conv_bias = jnp.sum(grad_conv, axis=(0, 1))
    grad_in_low = grad_conv_in.astype(jnp.bfloat16).reshape(row_count, local_width)
    grad_w_input = left_inner(normed, grad_in_low)
    grad_w_branch = left_inner(normed, grad_branch)
    mix_back_term = right_inner(grad_in_low, full_input) + right_inner(grad_branch, full_branch)
    grad_norm_mix = lax.psum(mix_back_term, "tp")
    grad_gain_mix = jnp.sum(grad_norm_mix * scaled_mix, axis=0)
    grad_tokens = (grad_resid + norm_back(grad_norm_mix, scaled_mix, scale_mix, gain_mix)).astype(
        jnp.bfloat16
    )
    owned = (
        lax.psum_scatter(grad_w_branch, "fsdp", scatter_dimension=0, tiled=True),
        lax.psum_scatter(grad_w_input, "fsdp", scatter_dimension=0, tiled=True),
        lax.psum_scatter(grad_w_gate, "fsdp", scatter_dimension=0, tiled=True),
        lax.psum_scatter(grad_w_up, "fsdp", scatter_dimension=0, tiled=True),
        lax.psum_scatter(grad_w_out, "fsdp", scatter_dimension=1, tiled=True),
        lax.psum_scatter(grad_w_down, "fsdp", scatter_dimension=1, tiled=True),
    )
    owned_branch, owned_input, owned_gate, owned_up, owned_out, owned_down = owned
    summed = lax.psum(
        (owned_branch, owned_input, owned_gate, owned_up, owned_out, owned_down), "ctx"
    )
    sum_branch, sum_input, sum_gate, sum_up, sum_out, sum_down = summed
    small_sums = lax.psum(
        (
            grad_gain_mix,
            grad_gain_mlp,
            grad_conv_weight,
            grad_conv_bias,
            grad_gate_a,
            grad_bias_a,
            grad_gate_x,
            grad_bias_x,
            grad_decay_param,
        ),
        ("fsdp", "ctx"),
    )
    (
        sum_gain_mix,
        sum_gain_mlp,
        sum_conv_weight,
        sum_conv_bias,
        sum_gate_a,
        sum_bias_a,
        sum_gate_x,
        sum_bias_x,
        sum_decay,
    ) = small_sums
    return (
        output.reshape(seq_count, tok_count, model_width),
        grad_tokens.reshape(seq_count, tok_count, model_width),
        sum_gain_mix,
        sum_branch,
        sum_input,
        sum_conv_weight,
        sum_conv_bias,
        sum_gate_a,
        sum_bias_a,
        sum_gate_x,
        sum_bias_x,
        sum_decay,
        sum_out,
        sum_gain_mlp,
        sum_gate,
        sum_up,
        sum_down,
    )


def solution(mesh):
    in_specs = (
        P("fsdp", "ctx", None),
        P("fsdp", None),
        P("fsdp", "ctx", None),
        P(),
        P("fsdp", "tp"),
        P("fsdp", "tp"),
        P(None, "tp"),
        P("tp"),
        P("tp", None, None),
        P("tp"),
        P("tp", None, None),
        P("tp"),
        P("tp"),
        P("tp", "fsdp"),
        P(),
        P("fsdp", "tp"),
        P("fsdp", "tp"),
        P("tp", "fsdp"),
    )
    out_specs = (
        P("fsdp", "ctx", None),
        P("fsdp", "ctx", None),
        P(),
        P("fsdp", "tp"),
        P("fsdp", "tp"),
        P(None, "tp"),
        P("tp"),
        P("tp", None, None),
        P("tp"),
        P("tp", None, None),
        P("tp"),
        P("tp"),
        P("tp", "fsdp"),
        P(),
        P("fsdp", "tp"),
        P("fsdp", "tp"),
        P("tp", "fsdp"),
    )
    return jax.shard_map(shards, mesh=mesh, in_specs=in_specs, out_specs=out_specs, check_vma=False)
```

profile of v0, /device:TPU:0, one launch (start us, length us, event | category | flops | bytes accessed | tf_op | source)
XLA Modules:
  0.0 3015.9 jit_solution(510944161602865288)
XLA Ops:
  13.5 53.5 %all-gather.7.cloned.1.call-done = bf16[2048,640]{1,0:T(8,128)(2,1)} async-done(((bf16[512,640]{1,0:T(8,128)(2,1)}), bf16[2048,640]{1,0:T(8,128)(2,1)}) %all-gather.7.cloned.1.call-update) | async-done | bytes 2621456 | tf_op jit(solution)/shard_map/all_gather | solution.py:90
  100.6 7.1 slice.691
  327.9 9.0 pad.269
  336.9 9.0 pad.270
  348.4 9.0 pad.289
  357.5 9.0 pad.290
  377.1 12.8 fusion.76
  390.0 8.9 fusion.138
  400.8 150.4 %all-reduce.93.cloned.1.call-done = f32[1024,2048]{1,0:T(8,128)} async-done(((f32[1024,2048]{1,0:T(8,128)}), f32[1024,2048]{1,0:T(8,128)}) %all-reduce.93.cloned.1.call-update) | async-done | bytes 8388624 | tf_op jit(solution)/shard_map/psum | solution.py:173
  563.1 105.0 %all-gather.13.cloned.1.call-done = bf16[2048,1536]{1,0:T(8,128)(2,1)} async-done(((bf16[512,1536]{1,0:T(8,128)(2,1)}), bf16[2048,1536]{1,0:T(8,128)(2,1)}) %all-gather.13.cloned.1.call-update) | async-done | bytes 6291472 | tf_op jit(solution)/shard_map/all_gather | solution.py:91
  668.1 12.2 fusion.139
  680.3 102.8 %all-gather.15.cloned.1.call-done = bf16[2048,1536]{1,0:T(8,128)(2,1)} async-done(((bf16[512,1536]{1,0:T(8,128)(2,1)}), bf16[2048,1536]{1,0:T(8,128)(2,1)}) %all-gather.15.cloned.1.call-update) | async-done | bytes 6291472 | tf_op jit(solution)/shard_map/all_gather | solution.py:92
  783.1 11.7 fusion.140
  794.8 103.4 %all-gather.17.cloned.1.call-done = bf16[1536,2048]{1,0:T(8,128)(2,1)} async-done(((bf16[1536,512]{1,0:T(8,128)(2,1)}), bf16[1536,2048]{1,0:T(8,128)(2,1)}) %all-gather.17.cloned.1.call-update) | async-done | bytes 6291472 | tf_op jit(solution)/shard_map/all_gather | solution.py:94
  898.2 18.2 multiply_convert_fusion.1
  916.5 10.0 fusion.142
  926.5 10.7 convolution_add_fusion.1
  937.2 151.2 %all-reduce.95.cloned.1.call-done = f32[1024,2048]{1,0:T(8,128)} async-done(((f32[1024,2048]{1,0:T(8,128)}), f32[1024,2048]{1,0:T(8,128)}) %all-reduce.95.cloned.1.call-update) | async-done | bytes 8388624 | tf_op jit(solution)/shard_map/psum | solution.py:192
  1088.4 7.6 multiply_reduce_fusion
  1112.3 7.1 slice.788
  1133.4 10.7 slice.789
  1144.2 10.7 slice.794
  1154.9 11.1 slice.787
  1166.0 12.5 fusion.54
  1178.4 20.8 reverse.9
  1333.4 8.7 fusion.115
  1402.3 9.2 pad.330
  1426.3 9.3 pad.310
  1441.6 9.2 pad.309
  1453.3 9.2 pad.329
  1478.5 20.8 rev.13
  1499.3 20.9 rev.12
  1520.3 7.1 multiply_reduce_fusion.3
  1545.1 8.9 fusion.44
  1568.8 12.6 fusion.145
  1581.6 12.5 fusion.146
  1594.1 12.2 fusion.30
  1606.4 12.1 fusion.141
  1632.6 29.5 reduce-scatter.9.cloned.1.call-done
  1662.1 214.6 %reduce-scatter.13.cloned.1.call-done = f32[512,1536]{1,0:T(8,128)} async-done(((f32[2048,1536]{1,0:T(8,128)}), f32[512,1536]{1,0:T(8,128)}) %reduce-scatter.13.cloned.1.call-update) | async-done | bytes 3145744 | tf_op jit(solution)/shard_map/reduce_scatter | solution.py:270
  1876.7 215.3 %reduce-scatter.15.cloned.1.call-done = f32[512,1536]{1,0:T(8,128)} async-done(((f32[2048,1536]{1,0:T(8,128)}), f32[512,1536]{1,0:T(8,128)}) %reduce-scatter.15.cloned.1.call-update) | async-done | bytes 3145744 | tf_op jit(solution)/shard_map/reduce_scatter | solution.py:271
  2092.0 215.2 %reduce-scatter.17.cloned.1.call-done = f32[1536,512]{1,0:T(8,128)} async-done(((f32[1536,2048]{1,0:T(8,128)}), f32[1536,512]{1,0:T(8,128)}) %reduce-scatter.17.cloned.1.call-update) | async-done | bytes 3145744 | tf_op jit(solution)/shard_map/reduce_scatter | solution.py:273
  2307.9 291.2 %all-reduce.99.cloned.1.call-done = (f32[1024,2048]{1,0:T(8,128)}, f32[1024,2048]{1,0:T(8,128)}) async-done(((f32[1024,2048]{1,0:T(8,128)}, f32[1024,2048]{1,0:T(8,128)}), (f32[1024,2048]{1,0:T(8,128)}, f32[1024,2048]{1,0:T(8,128)})) %all-reduce.99.cloned.1.call-update) | async-done | bytes 16777232 | tf_op jit(solution)/shard_map/psum | solution.py:182
  2604.9 39.3 %all-reduce.83 = (f32[2048]{0:T(1024)}, f32[4,640]{1,0:T(4,128)}, f32[640]{0:T(1024)}, f32[640]{0:T(1024)}, f32[640]{0:T(1024)}, /*index=5*/f32[640]{0:T(1024)}, f32[2048]{0:T(1024)}) all-reduce(f32[2048]{0:T(1024)S(1)} %get-tuple-element.283, ...), channel_id=1, replica_groups=mesh['fsdp'=4,'ctx'=2,'tp'=4] {'fsdp','ctx'}, use_global_device_ids=true, to_apply=%region_13.14 | all-reduce | flops 9216 | bytes 73728 | tf_op jit(solution)/shard_map/psum | solution.py:280
  2644.2 9.4 fusion.25
  2653.6 8.7 fusion.29
  2662.3 25.7 all-reduce.97.cloned.1.call-done
  2688.0 307.0 %all-reduce.101.cloned.1.call-done = (f32[512,640]{1,0:T(8,128)}, f32[512,640]{1,0:T(8,128)}, f32[640,512]{1,0:T(8,128)}, f32[512,1536]{1,0:T(8,128)}, f32[512,1536]{1,0:T(8,128)}, /*index=5*/f32[1536,512]{1,0:T(8,128)}) async-done(((f32[512,640]{1,0:T(8,128)}, f32[512,640]{1,0:T(8,128)}, f32[640,512]{1,0:T(8,128)}, f32[512,1536]{1,0:T(8,128)}, f32[512,1536]{1,0:T(8,128)}, ...) | async-done | bytes 13369360 | tf_op jit(solution)/shard_map/psum | solution.py:276
  (704 shorter events, 616.4 us)
Async XLA Ops:
  7.2 79.2 %copy-start = (bf16[4,160,160]{2,1,0:T(8,128)(2,1)S(1)}, bf16[4,160,160]{2,1,0:T(8,128)(2,1)}, u32[]{:S(2)}) copy-start(bf16[4,160,160]{2,1,0:T(8,128)(2,1)} %param.30) | copy-start | bytes 614404
  7.2 59.9 %all-gather.7.cloned.1.call-start = ((), (), s32[]{:S(2)}) async-start(), calls=%async_computation.6 | async-start | bytes 3276800 | tf_op jit(solution)/shard_map/all_gather | solution.py:90
  7.9 369.2 %all-gather.9.cloned.1.call-start = ((), (), s32[]{:S(2)}) async-start(), calls=%async_computation.7 | async-start | bytes 3276800 | tf_op jit(solution)/shard_map/all_gather | solution.py:89
  8.7 58.4 %copy-start.85 = (f32[2048]{0:T(1024)S(1)}, f32[2048]{0:T(1024)}, u32[]{:S(2)}) copy-start(f32[2048]{0:T(1024)} %param.25) | copy-start | bytes 24580
  8.7 381.2 %all-gather.11.cloned.1.call-start = ((), (), s32[]{:S(2)}) async-start(), calls=%async_computation.8 | async-start | bytes 3276800 | tf_op jit(solution)/shard_map/all_gather | solution.py:93
  9.5 541.8 %all-reduce.93.cloned.1.call-start = ((), (), s32[]{:S(2)}) async-start(), calls=%async_computation.9 | async-start | bytes 16777216 | tf_op jit(solution)/shard_map/psum | solution.py:173
  12.7 65.6 %copy-start.76 = (f32[640]{0:T(1024)}, f32[640]{0:T(1024)S(1)}, u32[]{:S(2)}) copy-start(f32[640]{0:T(1024)S(1)} %get-tuple-element.290) | copy-start | bytes 7684
  12.7 65.6 %copy-start.78 = (f32[640]{0:T(1024)}, f32[640]{0:T(1024)S(1)}, u32[]{:S(2)}) copy-start(f32[640]{0:T(1024)S(1)} %get-tuple-element.291) | copy-start | bytes 7684
  12.7 65.6 %copy-start.80 = (f32[640]{0:T(1024)}, f32[640]{0:T(1024)S(1)}, u32[]{:S(2)}) copy-start(f32[640]{0:T(1024)S(1)} %get-tuple-element.292) | copy-start | bytes 7684
  12.7 65.6 %copy-start.82 = (f32[640]{0:T(1024)}, f32[640]{0:T(1024)S(1)}, u32[]{:S(2)}) copy-start(f32[640]{0:T(1024)S(1)} %get-tuple-element.293) | copy-start | bytes 7684
  12.7 81.2 %copy-start.60 = (f32[640]{0:T(1024)}, f32[640]{0:T(1024)S(1)}, u32[]{:S(2)}) copy-start(f32[640]{0:T(1024)S(1)} %fusion.106) | copy-start | bytes 7684
  13.5 64.8 %copy-start.129 = (pred[1024]{0:T(1024)(128)(4,1)}, pred[1024]{0:T(1024)(128)(4,1)S(1)}, u32[]{:S(2)}) copy-start(pred[1024]{0:T(1024)(128)(4,1)S(1)} %get-tuple-element.295) | copy-start | bytes 3076
  13.5 64.8 %copy-start.131 = (pred[1024]{0:T(1024)(128)(4,1)}, pred[1024]{0:T(1024)(128)(4,1)S(1)}, u32[]{:S(2)}) copy-start(pred[1024]{0:T(1024)(128)(4,1)S(1)} %get-tuple-element.296) | copy-start | bytes 3076
  13.5 64.8 %copy-start.134 = (f32[640]{0:T(1024)S(1)}, f32[640]{0:T(1024)}, u32[]{:S(2)}) copy-start(f32[640]{0:T(1024)} %param.29) | copy-start | bytes 7684
  73.6 4.7 collective-permute-start
  357.5 19.6 copy-start.86
  398.9 269.3 %all-gather.13.cloned.1.call-start = ((), (), s32[]{:S(2)}) async-start(), calls=%async_computation.10 | async-start | bytes 7864320 | tf_op jit(solution)/shard_map/all_gather | solution.py:91
  399.5 383.6 %all-gather.15.cloned.1.call-start = ((), (), s32[]{:S(2)}) async-start(), calls=%async_computation.11 | async-start | bytes 7864320 | tf_op jit(solution)/shard_map/all_gather | solution.py:92
  400.0 498.2 %all-gather.17.cloned.1.call-start = ((), (), s32[]{:S(2)}) async-start(), calls=%async_computation.12 | async-start | bytes 7864320 | tf_op jit(solution)/shard_map/all_gather | solution.py:94
  400.8 159.6 %copy-start.65 = (f32[2048]{0:T(1024)S(1)}, f32[2048]{0:T(1024)}, u32[]{:S(2)}) copy-start(f32[2048]{0:T(1024)} %param.36) | copy-start | bytes 24580
  400.8 687.6 %all-reduce.95.cloned.1.call-start = ((), (), s32[]{:S(2)}) async-start(), calls=%async_computation.13 | async-start | bytes 16777216 | tf_op jit(solution)/shard_map/psum | solution.py:192
  937.2 695.4 %reduce-scatter.11.cloned.1.call-start = ((), (), s32[]{:S(2)}) async-start(), calls=%async_computation.16 | async-start | bytes 6553600 | tf_op jit(solution)/shard_map/reduce_scatter | solution.py:272
  1110.4 522.2 %reduce-scatter.7.cloned.1.call-start = ((), (), s32[]{:S(2)}) async-start(), calls=%async_computation.14 | async-start | bytes 6553600 | tf_op jit(solution)/shard_map/reduce_scatter | solution.py:268
  1313.8 19.1 copy-start.95
  1313.8 19.1 copy-start.96
  1313.8 19.1 copy-start.97
  1313.8 19.1 copy-start.98
  1313.9 19.1 copy-start.70
  1313.9 19.1 copy-start.71
  1313.9 19.3 copy-start.72
  1313.9 19.3 copy-start.73
  1313.9 19.4 copy-start.119
  1313.9 19.4 copy-start.117
  1342.2 319.9 %reduce-scatter.9.cloned.1.call-start = ((), (), s32[]{:S(2)}) async-start(), calls=%async_computation.15 | async-start | bytes 6553600 | tf_op jit(solution)/shard_map/reduce_scatter | solution.py:269
  1499.2 21.0 copy-start.6
  1499.2 21.0 copy-start.59
  1499.2 21.0 copy-start.61
  1499.2 21.0 copy-start.67
  1499.2 21.0 copy-start.69
  1499.3 21.0 copy-start.90
  1545.1 18.1 copy-start.3
  1554.1 5.6 collective-permute-start.1
  1568.8 307.9 %reduce-scatter.13.cloned.1.call-start = ((), (), s32[]{:S(2)}) async-start(), calls=%async_computation.17 | async-start | bytes 15728640 | tf_op jit(solution)/shard_map/reduce_scatter | solution.py:270
  1581.5 510.5 %reduce-scatter.15.cloned.1.call-start = ((), (), s32[]{:S(2)}) async-start(), calls=%async_computation.18 | async-start | bytes 15728640 | tf_op jit(solution)/shard_map/reduce_scatter | solution.py:271
  1594.1 713.1 %reduce-scatter.17.cloned.1.call-start = ((), (), s32[]{:S(2)}) async-start(), calls=%async_computation.19 | async-start | bytes 15728640 | tf_op jit(solution)/shard_map/reduce_scatter | solution.py:273
  1606.4 992.6 %all-reduce.99.cloned.1.call-start = ((), (), s32[]{:S(2)}) async-start(), calls=%async_computation.21 | async-start | bytes 33554432 | tf_op jit(solution)/shard_map/psum | solution.py:182
  1627.9 1060.1 %all-reduce.97.cloned.1.call-start = ((), (), s32[]{:S(2)}) async-start(), calls=%async_computation.20 | async-start | bytes 2621440 | tf_op jit(solution)/shard_map/psum | solution.py:280
  1632.5 1362.5 %all-reduce.101.cloned.1.call-start = ((), (), s32[]{:S(2)}) async-start(), calls=%async_computation.22 | async-start | bytes 26738688 | tf_op jit(solution)/shard_map/psum | solution.py:276
  (114 other events, 820.8 us)
Sparse Core Ops, SparseCore 0:
  9.6 57.4 all-gather.6
  68.6 53.5 all-gather.8
  123.8 53.4 all-gather.10
  399.0 152.1 all-reduce.92
  552.6 115.4 all-gather.12
  669.6 113.5 all-gather.14
  784.7 113.5 all-gather.16
  937.3 151.0 all-reduce.94
  1110.5 93.9 reduce-scatter.10
  1342.3 93.8 reduce-scatter.6
  1568.9 93.1 reduce-scatter.8
  1664.3 212.3 reduce-scatter.12
  1879.1 212.8 reduce-scatter.14
  2094.2 212.8 reduce-scatter.16
  2309.7 289.3 all-reduce.98
  2603.6 84.3 all-reduce.96
  2690.8 304.0 all-reduce.100
where the time goes:
time: 3040 us; the launch traced here: 3020 us
  waiting for transfers between devices  1970 us (65%)
  local copies, waits for them, and re-layouts  565 us (19%)
  other arithmetic  203 us (7%)
  matrix products  194 us (6%)
  blocking collectives  56.9 us (2%)
    psum x1, waiting for transfers between devices, shards(): lax.psum((owned_branch, owned_input, owned_gate, owned_up, owned_out, own...  307 us
    psum x1, waiting for transfers between devices, shards(): output = (resid_rows + lax.psum(down_term, 'tp')).astype(jnp.bfloat16)  291 us
    reduce_scatter x1, waiting for transfers between devices, shards(): lax.psum_scatter(grad_w_up, 'fsdp', scatter_dimension=0, tiled=True)  215 us
    reduce_scatter x1, waiting for transfers between devices, shards(): lax.psum_scatter(grad_w_down, 'fsdp', scatter_dimension=1, tiled=True)  215 us
    reduce_scatter x1, waiting for transfers between devices, shards(): lax.psum_scatter(grad_w_gate, 'fsdp', scatter_dimension=0, tiled=True)  215 us
    slice x70, local copies, waits for them, and re-layouts, shards(): lax.associative_scan(linear_combine, (jnp.flip(next_factor, 1), jnp.flip(...  170 us
    psum x1, waiting for transfers between devices, shards(): grad_norm_mlp = lax.psum(mlp_back_term, 'tp')  151 us
    psum x1, waiting for transfers between devices, shards(): resid_rows = inputs + lax.psum(mixer_term, 'tp')  150 us
  transfers between devices with their start and end apart: 19, of which 15 were waited for; matrix products, arithmetic and copies ran while one was open for 29% of the time, Pallas kernels for 0%

commit v1 on v0

--- a/solution.py
+++ b/solution.py
@@ -2,9 +2,11 @@
 import jax.numpy as jnp
 from jax import lax
 from jax.sharding import PartitionSpec as P
+from jax.lax import all_gather
 
 EPSILON = 1e-06
 RATE_SCALE = 8.0
+hold_paths = lambda array_in, along_axis: jnp.sum(all_gather(array_in, along_axis), axis=0)
 
 
 def passed_along(block, axis, distance):
@@ -179,7 +181,7 @@
     gate_act, gate_slope = gelu_slope(gate_pre)
     hidden = (gate_act * up_pre).astype(jnp.bfloat16)
     down_term = matmul(hidden, full_down)
-    output = (resid_rows + lax.psum(down_term, "tp")).astype(jnp.bfloat16)
+    output = (resid_rows + hold_paths(down_term, "tp")).astype(jnp.bfloat16)
     grad_low = cotangent.reshape(row_count, model_width)
     grad_out = grad_low.astype(jnp.float32)
     grad_w_down = left_inner(hidden, grad_low)

time: 3040 us -> 2760 us (0.908)
  waiting for transfers between devices: 1970 us -> 1740 us
  local copies, waits for them, and re-layouts: 565 us -> 522 us
    reduce_scatter x1, waiting for transfers between devices: 215 us -> 0.02 us  [shards(): lax.psum_scatter(grad_w_up, 'fsdp', scatter_dimension=0, tiled=True)]
    reduce_scatter x1, waiting for transfers between devices: 215 us -> 0.02 us  [shards(): lax.psum_scatter(grad_w_gate, 'fsdp', scatter_dimension=0, tiled=True)]
    all_gather x0 -> x1, waiting for transfers between devices: none -> 196 us  [all_gather(array_in, along_axis)]
    psum x1, waiting for transfers between devices: 291 us -> 155 us  [shards(): grad_norm_mix = lax.psum(mix_back_term, 'tp')]
    reduce_scatter x1, waiting for transfers between devices: 0.02 us -> 97.2 us  [shards(): lax.psum_scatter(grad_w_out, 'fsdp', scatter_dimension=1, tiled=True)]
    reduce_scatter x1, waiting for transfers between devices: 0.02 us -> 96.5 us  [shards(): lax.psum_scatter(grad_w_branch, 'fsdp', scatter_dimension=0, tiled=True)]
    reduce_scatter x1, waiting for transfers between devices: 215 us -> 131 us  [shards(): lax.psum_scatter(grad_w_down, 'fsdp', scatter_dimension=1, tiled=True)]
    reduce_scatter x1, waiting for transfers between devices: 29.5 us -> 96.5 us  [shards(): lax.psum_scatter(grad_w_input, 'fsdp', scatter_dimension=0, tiled=True)]
  transfers between devices with their start and end apart: 19 -> 20, of which waited for: 15 -> 16; matrix products, arithmetic and copies ran while one was open for 29% -> 31% of each run, Pallas kernels for 0% -> 0%
where the time goes in v1:
time: 2760 us; the launch traced here: 2740 us
  waiting for transfers between devices  1740 us (63%)
  local copies, waits for them, and re-layouts  522 us (19%)
  other arithmetic  203 us (7%)
  matrix products  193 us (7%)
  blocking collectives  56.8 us (2%)
    psum x1, waiting for transfers between devices, shards(): lax.psum((owned_branch, owned_input, owned_gate, owned_up, owned_out, own...  307 us
    all_gather x1, waiting for transfers between devices, all_gather(array_in, along_axis)  196 us
    slice x70, local copies, waits for them, and re-layouts, shards(): lax.associative_scan(linear_combine, (jnp.flip(next_factor, 1), jnp.flip(...  171 us
    psum x1, waiting for transfers between devices, shards(): grad_norm_mix = lax.psum(mix_back_term, 'tp')  155 us
    psum x1, waiting for transfers between devices, shards(): resid_rows = inputs + lax.psum(mixer_term, 'tp')  150 us
    reduce_scatter x1, waiting for transfers between devices, shards(): lax.psum_scatter(grad_w_down, 'fsdp', scatter_dimension=1, tiled=True)  131 us
    slice x68, local copies, waits for them, and re-layouts, shards(): lax.associative_scan(linear_combine, (carry_factor, driven), axis=1)  130 us
    all_gather x1, waiting for transfers between devices, shards(): lax.all_gather(w_gate, 'fsdp', axis=0, tiled=True)  105 us
  transfers between devices with their start and end apart: 20, of which 16 were waited for; matrix products, arithmetic and copies ran while one was open for 31% of the time, Pallas kernels for 0%

profile of v1, /device:TPU:0, one launch (start us, length us, event | category | flops | bytes accessed | tf_op | source)
XLA Modules:
  0.0 2736.5 jit_solution(11645129124524112211)
XLA Ops:
  13.6 53.5 %all-gather.9.cloned.1.call-done = bf16[2048,640]{1,0:T(8,128)(2,1)} async-done(((bf16[512,640]{1,0:T(8,128)(2,1)}), bf16[2048,640]{1,0:T(8,128)(2,1)}) %all-gather.9.cloned.1.call-update) | async-done | bytes 2621456 | tf_op jit(solution)/shard_map/all_gather | solution.py:92
  100.4 7.1 slice.691
  241.4 7.0 slice.762
  316.2 12.4 fusion.76
  328.6 7.8 fusion.138
  338.4 150.4 %all-reduce.92.cloned.1.call-done = f32[1024,2048]{1,0:T(8,128)} async-done(((f32[1024,2048]{1,0:T(8,128)}), f32[1024,2048]{1,0:T(8,128)}) %all-reduce.92.cloned.1.call-update) | async-done | bytes 8388624 | tf_op jit(solution)/shard_map/psum | solution.py:175
  500.7 105.0 %all-gather.15.cloned.1.call-done = bf16[2048,1536]{1,0:T(8,128)(2,1)} async-done(((bf16[512,1536]{1,0:T(8,128)(2,1)}), bf16[2048,1536]{1,0:T(8,128)(2,1)}) %all-gather.15.cloned.1.call-update) | async-done | bytes 6291472 | tf_op jit(solution)/shard_map/all_gather | solution.py:93
  605.7 11.8 fusion.139
  617.6 103.1 %all-gather.17.cloned.1.call-done = bf16[2048,1536]{1,0:T(8,128)(2,1)} async-done(((bf16[512,1536]{1,0:T(8,128)(2,1)}), bf16[2048,1536]{1,0:T(8,128)(2,1)}) %all-gather.17.cloned.1.call-update) | async-done | bytes 6291472 | tf_op jit(solution)/shard_map/all_gather | solution.py:94
  720.7 11.7 fusion.140
  732.4 103.4 %all-gather.19.cloned.1.call-done = bf16[1536,2048]{1,0:T(8,128)(2,1)} async-done(((bf16[1536,512]{1,0:T(8,128)(2,1)}), bf16[1536,2048]{1,0:T(8,128)(2,1)}) %all-gather.19.cloned.1.call-update) | async-done | bytes 6291472 | tf_op jit(solution)/shard_map/all_gather | solution.py:96
  835.8 17.7 multiply_convert_fusion.1
  853.5 10.0 fusion.142
  863.6 10.9 convolution_add_fusion.1
  874.5 10.9 fusion.141
  885.5 12.6 fusion.145
  898.1 12.6 fusion.146
  910.8 12.2 fusion.30
  923.1 102.6 %all-reduce.94.cloned.1.call-done = f32[1024,2048]{1,0:T(8,128)} async-done(((f32[1024,2048]{1,0:T(8,128)}), f32[1024,2048]{1,0:T(8,128)}) %all-reduce.94.cloned.1.call-update) | async-done | bytes 8388624 | tf_op jit(solution)/shard_map/psum | solution.py:194
  1025.7 7.5 multiply_reduce_fusion
  1033.2 195.7 %all-gather.21.cloned.1.call-done = f32[4096,2048]{1,0:T(8,128)} async-done(((f32[1024,2048]{1,0:T(8,128)}), f32[4096,2048]{1,0:T(8,128)}) %all-gather.21.cloned.1.call-update) | async-done | bytes 33554448 | tf_op jit(solution)/shard_map/all_gather | solution.py:9
  1228.9 17.1 reduce_sum.137
  1246.0 13.1 multiply_add_fusion
  1270.7 7.1 slice.788
  1291.9 10.8 slice.789
  1302.6 10.7 slice.794
  1313.3 11.0 slice.787
  1324.3 12.7 fusion.54
  1337.1 20.7 reverse.9
  1484.1 7.0 slice.862
  1492.4 8.7 fusion.115
  1561.0 9.0 pad.330
  1584.7 9.0 pad.310
  1599.6 9.1 pad.309
  1611.2 9.0 pad.329
  1636.5 20.7 rev.13
  1657.2 20.9 rev.12
  1678.2 7.3 multiply_reduce_fusion.3
  1703.1 8.8 fusion.44
  1742.9 130.6 %reduce-scatter.17.cloned.1.call-done = f32[1536,512]{1,0:T(8,128)} async-done(((f32[1536,2048]{1,0:T(8,128)}), f32[1536,512]{1,0:T(8,128)}) %reduce-scatter.17.cloned.1.call-update) | async-done | bytes 3145744 | tf_op jit(solution)/shard_map/reduce_scatter | solution.py:275
  1873.5 97.2 %reduce-scatter.11.cloned.1.call-done = f32[640,512]{1,0:T(8,128)} async-done(((f32[640,2048]{1,0:T(8,128)}), f32[640,512]{1,0:T(8,128)}) %reduce-scatter.11.cloned.1.call-update) | async-done | bytes 1310736 | tf_op jit(solution)/shard_map/reduce_scatter | solution.py:274
  1970.7 96.5 %reduce-scatter.7.cloned.1.call-done = f32[512,640]{1,0:T(8,128)} async-done(((f32[2048,640]{1,0:T(8,128)}), f32[512,640]{1,0:T(8,128)}) %reduce-scatter.7.cloned.1.call-update) | async-done | bytes 1310736 | tf_op jit(solution)/shard_map/reduce_scatter | solution.py:270
  2067.1 96.5 %reduce-scatter.9.cloned.1.call-done = f32[512,640]{1,0:T(8,128)} async-done(((f32[2048,640]{1,0:T(8,128)}), f32[512,640]{1,0:T(8,128)}) %reduce-scatter.9.cloned.1.call-update) | async-done | bytes 1310736 | tf_op jit(solution)/shard_map/reduce_scatter | solution.py:271
  2164.3 155.0 %all-reduce.96.cloned.1.call-done = f32[1024,2048]{1,0:T(8,128)} async-done(((f32[1024,2048]{1,0:T(8,128)}), f32[1024,2048]{1,0:T(8,128)}) %all-reduce.96.cloned.1.call-update) | async-done | bytes 8388624 | tf_op jit(solution)/shard_map/psum | solution.py:264
  2325.2 39.2 %all-reduce.83 = (f32[2048]{0:T(1024)}, f32[4,640]{1,0:T(4,128)}, f32[640]{0:T(1024)}, f32[640]{0:T(1024)}, f32[640]{0:T(1024)}, /*index=5*/f32[640]{0:T(1024)}, f32[2048]{0:T(1024)}) all-reduce(f32[2048]{0:T(1024)S(1)} %get-tuple-element.283, ...), channel_id=1, replica_groups=mesh['fsdp'=4,'ctx'=2,'tp'=4] {'fsdp','ctx'}, use_global_device_ids=true, to_apply=%region_13.14 | all-reduce | flops 9216 | bytes 73728 | tf_op jit(solution)/shard_map/psum | solution.py:282
  2364.4 10.3 fusion.29
  2374.8 33.6 %all-reduce.98.cloned.1.call-done = (f32[4,160,160]{2,1,0:T(8,128)}, f32[4,160,160]{2,1,0:T(8,128)}) async-done(((f32[4,160,160]{2,1,0:T(8,128)}, f32[4,160,160]{2,1,0:T(8,128)}), (f32[4,160,160]{2,1,0:T(8,128)}, f32[4,160,160]{2,1,0:T(8,128)})) %all-reduce.98.cloned.1.call-update) | async-done | bytes 819216 | tf_op jit(solution)/shard_map/psum | solution.py:282
  2408.4 307.0 %all-reduce.100.cloned.1.call-done = (f32[512,640]{1,0:T(8,128)}, f32[512,640]{1,0:T(8,128)}, f32[640,512]{1,0:T(8,128)}, f32[512,1536]{1,0:T(8,128)}, f32[512,1536]{1,0:T(8,128)}, /*index=5*/f32[1536,512]{1,0:T(8,128)}) async-done(((f32[512,640]{1,0:T(8,128)}, f32[512,640]{1,0:T(8,128)}, f32[640,512]{1,0:T(8,128)}, f32[512,1536]{1,0:T(8,128)}, f32[512,1536]{1,0:T(8,128)}, ...) | async-done | bytes 13369360 | tf_op jit(solution)/shard_map/psum | solution.py:278
  (681 shorter events, 575.3 us)
Async XLA Ops:
  7.2 79.0 %copy-start = (bf16[4,160,160]{2,1,0:T(8,128)(2,1)S(1)}, bf16[4,160,160]{2,1,0:T(8,128)(2,1)}, u32[]{:S(2)}) copy-start(bf16[4,160,160]{2,1,0:T(8,128)(2,1)} %param.30) | copy-start | bytes 614404
  7.2 59.9 %all-gather.9.cloned.1.call-start = ((), (), s32[]{:S(2)}) async-start(), calls=%async_computation.6 | async-start | bytes 3276800 | tf_op jit(solution)/shard_map/all_gather | solution.py:92
  7.9 308.2 %all-gather.11.cloned.1.call-start = ((), (), s32[]{:S(2)}) async-start(), calls=%async_computation.7 | async-start | bytes 3276800 | tf_op jit(solution)/shard_map/all_gather | solution.py:91
  8.7 58.4 %copy-start.79 = (f32[2048]{0:T(1024)S(1)}, f32[2048]{0:T(1024)}, u32[]{:S(2)}) copy-start(f32[2048]{0:T(1024)} %param.25) | copy-start | bytes 24580
  8.7 319.9 %all-gather.13.cloned.1.call-start = ((), (), s32[]{:S(2)}) async-start(), calls=%async_computation.8 | async-start | bytes 3276800 | tf_op jit(solution)/shard_map/all_gather | solution.py:95
  9.5 479.3 %all-reduce.92.cloned.1.call-start = ((), (), s32[]{:S(2)}) async-start(), calls=%async_computation.9 | async-start | bytes 16777216 | tf_op jit(solution)/shard_map/psum | solution.py:175
  12.6 303.6 %copy-start.76 = (f32[1024]{0:T(1024)}, f32[1024]{0:T(1024)S(1)}, u32[]{:S(2)}) copy-start(f32[1024]{0:T(1024)S(1)} %add_rsqrt_fusion.1) | copy-start | bytes 12292
  12.7 65.6 %copy-start.68 = (f32[640]{0:T(1024)}, f32[640]{0:T(1024)S(1)}, u32[]{:S(2)}) copy-start(f32[640]{0:T(1024)S(1)} %get-tuple-element.290) | copy-start | bytes 7684
  12.7 65.6 %copy-start.70 = (f32[640]{0:T(1024)}, f32[640]{0:T(1024)S(1)}, u32[]{:S(2)}) copy-start(f32[640]{0:T(1024)S(1)} %get-tuple-element.291) | copy-start | bytes 7684
  12.7 65.6 %copy-start.72 = (f32[640]{0:T(1024)}, f32[640]{0:T(1024)S(1)}, u32[]{:S(2)}) copy-start(f32[640]{0:T(1024)S(1)} %get-tuple-element.292) | copy-start | bytes 7684
  12.7 65.6 %copy-start.74 = (f32[640]{0:T(1024)}, f32[640]{0:T(1024)S(1)}, u32[]{:S(2)}) copy-start(f32[640]{0:T(1024)S(1)} %get-tuple-element.293) | copy-start | bytes 7684
  12.8 81.0 %copy-start.56 = (f32[640]{0:T(1024)}, f32[640]{0:T(1024)S(1)}, u32[]{:S(2)}) copy-start(f32[640]{0:T(1024)S(1)} %fusion.106) | copy-start | bytes 7684
  13.6 64.8 %copy-start.117 = (pred[1024]{0:T(1024)(128)(4,1)}, pred[1024]{0:T(1024)(128)(4,1)S(1)}, u32[]{:S(2)}) copy-start(pred[1024]{0:T(1024)(128)(4,1)S(1)} %get-tuple-element.295) | copy-start | bytes 3076
  13.6 64.8 %copy-start.119 = (pred[1024]{0:T(1024)(128)(4,1)}, pred[1024]{0:T(1024)(128)(4,1)S(1)}, u32[]{:S(2)}) copy-start(pred[1024]{0:T(1024)(128)(4,1)S(1)} %get-tuple-element.296) | copy-start | bytes 3076
  13.6 64.8 %copy-start.122 = (f32[640]{0:T(1024)S(1)}, f32[640]{0:T(1024)}, u32[]{:S(2)}) copy-start(f32[640]{0:T(1024)} %param.29) | copy-start | bytes 7684
  73.6 4.7 collective-permute-start
  336.4 269.3 %all-gather.15.cloned.1.call-start = ((), (), s32[]{:S(2)}) async-start(), calls=%async_computation.10 | async-start | bytes 7864320 | tf_op jit(solution)/shard_map/all_gather | solution.py:93
  337.0 383.7 %all-gather.17.cloned.1.call-start = ((), (), s32[]{:S(2)}) async-start(), calls=%async_computation.11 | async-start | bytes 7864320 | tf_op jit(solution)/shard_map/all_gather | solution.py:94
  337.6 498.2 %all-gather.19.cloned.1.call-start = ((), (), s32[]{:S(2)}) async-start(), calls=%async_computation.12 | async-start | bytes 7864320 | tf_op jit(solution)/shard_map/all_gather | solution.py:96
  338.4 159.6 %copy-start.59 = (f32[2048]{0:T(1024)S(1)}, f32[2048]{0:T(1024)}, u32[]{:S(2)}) copy-start(f32[2048]{0:T(1024)} %param.36) | copy-start | bytes 24580
  338.4 687.3 %all-reduce.94.cloned.1.call-start = ((), (), s32[]{:S(2)}) async-start(), calls=%async_computation.13 | async-start | bytes 16777216 | tf_op jit(solution)/shard_map/psum | solution.py:194
  874.4 354.5 %all-gather.21.cloned.1.call-start = ((), (), s32[]{:S(2)}) async-start(), calls=%async_computation.21 | async-start | bytes 41943040 | tf_op jit(solution)/shard_map/all_gather | solution.py:9
  885.4 857.4 %reduce-scatter.13.cloned.1.call-start = ((), (), s32[]{:S(2)}) async-start(), calls=%async_computation.18 | async-start | bytes 15728640 | tf_op jit(solution)/shard_map/reduce_scatter | solution.py:272
  898.1 844.8 %reduce-scatter.15.cloned.1.call-start = ((), (), s32[]{:S(2)}) async-start(), calls=%async_computation.19 | async-start | bytes 15728640 | tf_op jit(solution)/shard_map/reduce_scatter | solution.py:273
  910.7 962.8 %reduce-scatter.17.cloned.1.call-start = ((), (), s32[]{:S(2)}) async-start(), calls=%async_computation.20 | async-start | bytes 15728640 | tf_op jit(solution)/shard_map/reduce_scatter | solution.py:275
  923.0 1047.6 %reduce-scatter.11.cloned.1.call-start = ((), (), s32[]{:S(2)}) async-start(), calls=%async_computation.17 | async-start | bytes 6553600 | tf_op jit(solution)/shard_map/reduce_scatter | solution.py:274
  1267.2 799.9 %reduce-scatter.7.cloned.1.call-start = ((), (), s32[]{:S(2)}) async-start(), calls=%async_computation.15 | async-start | bytes 6553600 | tf_op jit(solution)/shard_map/reduce_scatter | solution.py:270
  1472.8 19.1 copy-start.89
  1472.8 19.1 copy-start.90
  1472.8 19.1 copy-start.91
  1472.8 19.2 copy-start.64
  1472.8 19.2 copy-start.65
  1472.8 19.4 copy-start.66
  1472.8 19.4 copy-start.67
  1472.8 19.4 copy-start.110
  1472.9 19.4 copy-start.109
  1501.1 662.5 %reduce-scatter.9.cloned.1.call-start = ((), (), s32[]{:S(2)}) async-start(), calls=%async_computation.16 | async-start | bytes 6553600 | tf_op jit(solution)/shard_map/reduce_scatter | solution.py:271
  1657.2 20.9 copy-start.5
  1657.2 20.9 copy-start.55
  1657.2 20.9 copy-start.57
  1657.2 20.9 copy-start.61
  1657.2 20.9 copy-start.63
  1657.2 20.9 copy-start.84
  1712.0 5.6 collective-permute-start.1
  1726.6 592.7 %all-reduce.96.cloned.1.call-start = ((), (), s32[]{:S(2)}) async-start(), calls=%async_computation.14 | async-start | bytes 16777216 | tf_op jit(solution)/shard_map/psum | solution.py:264
  1738.2 670.1 %all-reduce.98.cloned.1.call-start = ((), (), s32[]{:S(2)}) async-start(), calls=%async_computation.22 | async-start | bytes 2621440 | tf_op jit(solution)/shard_map/psum | solution.py:282
  1742.8 972.5 %all-reduce.100.cloned.1.call-start = ((), (), s32[]{:S(2)}) async-start(), calls=%async_computation.23 | async-start | bytes 26738688 | tf_op jit(solution)/shard_map/psum | solution.py:278
  2164.3 160.9 %copy-start.78 = (f32[2048]{0:T(1024)S(1)}, f32[2048]{0:T(1024)}, u32[]{:S(2)}) copy-start(f32[2048]{0:T(1024)} %get-tuple-element.281) | copy-start | bytes 24580
  (102 other events, 634.3 us)
Sparse Core Ops, SparseCore 0:
  9.6 57.4 all-gather.8
  68.6 53.5 all-gather.10
  123.8 53.4 all-gather.12
  336.6 152.2 all-reduce.91
  490.2 115.4 all-gather.14
  607.2 113.5 all-gather.16
  722.3 113.5 all-gather.18
  874.6 151.0 all-reduce.93
  1027.2 201.6 all-gather.20
  1231.1 211.8 reduce-scatter.12
  1445.4 212.9 reduce-scatter.14
  1660.6 212.8 reduce-scatter.16
  1875.8 94.8 reduce-scatter.10
  1972.8 94.2 reduce-scatter.6
  2069.3 94.2 reduce-scatter.8
  2165.9 153.3 all-reduce.95
  2323.9 84.3 all-reduce.97
  2411.2 304.0 all-reduce.99
